TPU v7x, 32 devices: a whole 2x2x4 slice. The times are simulated.
32 devices in a mesh: region: 2 (over x), owner: 16 (over z, y, core).
Axes of the slice: x: 2, y: 2, z: 4, core: 2. Of those that a mesh axis runs over, the one named last changes fastest.
Arguments:
- voxels: bfloat16 [2, 16, 1, 256, 1024], P('region', 'owner'), may hold values from -6 to 6
- norm_gain: float32 [1024], replicated, may hold values from 0.5 to 1.5
- qkv_weight: bfloat16 [1024, 3072], P(('region', 'owner')), may hold values from -0.14453125 to 0.14453125
- out_weight: bfloat16 [1024, 1024], P(('region', 'owner')), may hold values from -0.1875 to 0.1875
- neighbours: int32 [2, 16, 1, 8], P('region', 'owner'), may hold values from -1 to 31, as said below
Outputs:
- attended_voxels: bfloat16 [2, 16, 1, 256, 1024], P('region', 'owner')
Inputs may be any that keep to these rules, and one draw needn't show every extreme that they name: `neighbours`: each entry is -1 or the number (r * 16 + o) + c of a block c held by the device at region r and owner o, where r and o each differ by at most one from those of the list's own block; a list never names its own block and names no block twice.
All inputs are finite; a program needn't handle non-finite values.
Results may differ from a plain program's by a relative error of at most 0.0057.
Values may be sent and summed in bfloat16 or wider, within the bound.
A program may use at most 64 MiB of HBM per device.

v0:
```python
import jax
import jax.numpy as jnp
from jax import lax
from jax.sharding import PartitionSpec as P

HEAD_DIM = 64


def padded(value, sides, width):
    for axis, dim in sides:
        devices, length = (lax.axis_size(axis), value.shape[dim])
        up = [(i, (i + 1) % devices) for i in range(devices - 1)]
        down = [(j, i) for i, j in up]
        last = lax.slice_in_dim(value, length - width, length, axis=dim)
        first = lax.slice_in_dim(value, 0, width, axis=dim)
        before = lax.ppermute(last, axis, up)
        after = lax.ppermute(first, axis, down)
        value = jnp.concatenate([before, value, after], axis=dim)
    return value


def layer_norm(inputs, norm_gain):
    widened = inputs.astype(jnp.float32)
    average = jnp.mean(widened, axis=-1, keepdims=True)
    spread = jnp.mean((widened - average) ** 2, axis=-1, keepdims=True)
    return ((widened - average) * lax.rsqrt(spread + 1e-06) * norm_gain).astype(jnp.bfloat16)


def shards(voxels, norm_gain, qkv_weight, out_weight, neighbours):
    capacity = voxels.shape[2]
    block_size = voxels.shape[3]
    model_width = voxels.shape[4]
    token_count = capacity * block_size
    flat_tokens = voxels.reshape(token_count, model_width)
    normed = layer_norm(flat_tokens, norm_gain)
    columns = normed
    qkv = jnp.dot(
        columns,
        lax.all_gather(qkv_weight, ("region", "owner"), axis=0, tiled=True),
        preferred_element_type=jnp.float32,
    )
    qkv = qkv.astype(jnp.bfloat16)
    queries = qkv[:, :model_width].reshape(capacity, block_size, model_width)
    kv_pairs = qkv[:, model_width:].reshape(1, 1, capacity, block_size, 2 * model_width)
    widened_pairs = padded(kv_pairs, (("owner", 1),), 1)
    extended = padded(widened_pairs, (("region", 0),), 1)
    extended = extended.reshape(9 * capacity * block_size, 2 * model_width)
    key_rows = extended[:, :model_width]
    value_rows = extended[:, model_width:]
    owner_count = lax.axis_size("owner")
    my_region = lax.axis_index("region")
    my_owner = lax.axis_index("owner")
    list_ids = neighbours.reshape(capacity, neighbours.shape[-1])
    far_region = list_ids // (owner_count * capacity)
    far_owner = list_ids // capacity % owner_count
    far_slot = list_ids % capacity
    local_ids = (
        (far_region - my_region + 1) * 3 + (far_owner - my_owner + 1)
    ) * capacity + far_slot
    local_ids = jnp.where(list_ids >= 0, local_ids, -1)
    slot_ids = jnp.arange(9 * capacity, dtype=jnp.int32)
    listed = jnp.any(local_ids[:, :, None] == slot_ids[None, None, :], axis=1)
    own_block = slot_ids[None, :] == (4 * capacity + jnp.arange(capacity, dtype=jnp.int32))[:, None]
    allowed = listed | own_block
    key_mask = jnp.repeat(allowed, block_size, axis=1)
    group_heads = 2
    group_cols = group_heads * HEAD_DIM
    group_count = model_width // group_cols
    score_scale = HEAD_DIM ** (-0.5)

    def attend_group(group_idx, buffer):
        offset = group_idx * group_cols
        query_part = lax.dynamic_slice_in_dim(queries, offset, group_cols, 2).reshape(
            capacity, block_size, group_heads, HEAD_DIM
        )
        key_part = lax.dynamic_slice_in_dim(key_rows, offset, group_cols, 1).reshape(
            -1, group_heads, HEAD_DIM
        )
        value_part = lax.dynamic_slice_in_dim(value_rows, offset, group_cols, 1).reshape(
            -1, group_heads, HEAD_DIM
        )
        scores = (
            jnp.einsum("cshd,khd->chsk", query_part, key_part, preferred_element_type=jnp.float32)
            * score_scale
        )
        scores = jnp.where(key_mask[:, None, None, :], scores, -1e30)
        row_max = jnp.max(scores, axis=-1, keepdims=True)
        shifted = jnp.exp(scores - row_max)
        attn_probs = (shifted / jnp.sum(shifted, axis=-1, keepdims=True)).astype(jnp.bfloat16)
        attended = jnp.einsum(
            "chsk,khd->cshd", attn_probs, value_part, preferred_element_type=jnp.float32
        )
        attended = attended.astype(jnp.bfloat16).reshape(capacity, block_size, group_cols)
        return lax.dynamic_update_slice_in_dim(buffer, attended, offset, 2)

    mixed = lax.fori_loop(
        0, group_count, attend_group, jnp.zeros((capacity, block_size, model_width), jnp.bfloat16)
    )
    mixed_rows = mixed.reshape(token_count, model_width)
    columns = mixed_rows
    projected = jnp.dot(
        columns,
        lax.all_gather(out_weight, ("region", "owner"), axis=0, tiled=True),
        preferred_element_type=jnp.float32,
    )
    result = flat_tokens.astype(jnp.float32) + projected
    return result.astype(jnp.bfloat16).reshape(voxels.shape)


def solution(mesh):
    return jax.shard_map(
        shards,
        mesh=mesh,
        in_specs=(
            P("region", "owner", None, None, None),
            P(),
            P(("region", "owner"), None),
            P(("region", "owner"), None),
            P("region", "owner", None, None),
        ),
        out_specs=P("region", "owner", None, None, None),
        check_vma=False,
    )
```

profile of v0, /device:TPU:4, one launch (start us, length us, event | category | flops | bytes accessed | tf_op | source)
XLA Modules:
  0.0 295.9 jit_solution(13152737129808272242)
XLA Ops:
  9.8 70.9 %all-gather.3.cloned.1.call-done = bf16[1024,3072]{1,0:T(8,128)(2,1)} async-done(((bf16[32,3072]{1,0:T(8,128)(2,1)}), bf16[1024,3072]{1,0:T(8,128)(2,1)}) %all-gather.3.cloned.1.call-update) | async-done | bytes 6291472 | tf_op jit(solution)/shard_map/all_gather | solution.py:39
  80.7 4.9 %convolution_convert_fusion = bf16[256,3072]{1,0:T(8,128)(2,1)S(1)} fusion(bf16[1024,3072]{1,0:T(8,128)(2,1)} %all-gather.3.cloned.1.call-done, bf16[1,1,1,256,1024]{4,3,2,1,0:T(8,128)(2,1)} %param.7, f32[1024]{0:T(1024)} %param.8, f32[256]{0:T(256)S(1)} %add_rsqrt_fusion, f32[256]{0:T(256)S(1)} %broadcast_multiply_fusion), kind=kOutput, calls=%fused_computation.17 | convolution fusion | flops 1612709888 | bytes 8394752 | tf_op jit(solution)/shard_map/dot_general | solution.py:37
  87.9 3.4 %collective-permute-start.1 = (bf16[1,1,1,256,2048]{4,3,2,1,0:T(8,128)(2,1)S(1)}, bf16[1,1,1,256,2048]{4,3,2,1,0:T(8,128)(2,1)S(1)}, u32[]{:S(2)}, u32[]{:S(2)}) collective-permute-start(bf16[1,1,1,256,2048]{4,3,2,1,0:T(8,128)(2,1)S(1)} %slice_bitcast_fusion), channel_id=1, source_target_pairs={{1,0},{2,1},{3,2},{4,3},{5,4},{6,5},{7,6},{8,7},{9,8},{10,9},{11,1... | collective-permute-start | bytes 3145736 | tf_op jit(solution)/shard_map/ppermute | solution.py:17
  91.3 21.8 %collective-permute-done = bf16[1,1,1,256,2048]{4,3,2,1,0:T(8,128)(2,1)S(1)} collective-permute-done((bf16[1,1,1,256,2048]{4,3,2,1,0:T(8,128)(2,1)S(1)}, bf16[1,1,1,256,2048]{4,3,2,1,0:T(8,128)(2,1)S(1)}, u32[]{:S(2)}, u32[]{:S(2)}) %collective-permute-start) | collective-permute-done | bytes 1048608 | tf_op jit(solution)/shard_map/ppermute | solution.py:16
  113.1 2.3 pad_maximum_fusion.1
  115.4 2.7 collective-permute-start.2
  121.4 64.2 %collective-permute-done.2 = bf16[1,3,1,256,2048]{4,3,2,1,0:T(8,128)(2,1)S(1)} collective-permute-done((bf16[1,3,1,256,2048]{4,3,2,1,0:T(8,128)(2,1)}, bf16[1,3,1,256,2048]{4,3,2,1,0:T(8,128)(2,1)S(1)}, u32[]{:S(2)}, u32[]{:S(2)}) %collective-permute-start.2) | collective-permute-done | bytes 3145760 | tf_op jit(solution)/shard_map/ppermute | solution.py:16
  187.3 2.6 collective-permute-done.3
  189.9 4.7 %pad_maximum_fusion = bf16[3,3,1,256,2048]{4,3,2,1,0:T(8,128)(2,1)S(1)} fusion(bf16[1,3,1,256,2048]{4,3,2,1,0:T(8,128)(2,1)} %collective-permute-done.3, bf16[1,1,1,256,2048]{4,3,2,1,0:T(8,128)(2,1)} %copy-done.4, bf16[1,1,1,256,2048]{4,3,2,1,0:T(8,128)(2,1)} %copy-done.1, bf16[1,1,1,256,2048]{4,3,2,1,0:T(8,128)(2,1)} %copy-done.3, ...), kind=kLoop, calls=%fused_computation.16 | loop fusion | flops 18874368 | bytes 18874368 | tf_op jit(solution)/shard_map/concatenate | solution.py:18
  194.5 4.8 %fusion.28 = (bf16[2304,1024]{1,0:T(8,128)(2,1)}, bf16[2304,1024]{1,0:T(8,128)(2,1)}) fusion(bf16[2304,2048]{1,0:T(8,128)(2,1)S(1)} %bitcast.104), kind=kLoop, calls=%fused_computation.51 | loop fusion | bytes 18874368 | tf_op jit(solution)/shard_map/slice | solution.py:48
  199.4 86.6 %while.14 = (s32[]{:T(128)}, bf16[1,256,1024]{1,2,0:T(8,128)(2,1)S(1)}, bf16[2304,1024]{1,0:T(8,128)(2,1)}, bf16[2304,1024]{1,0:T(8,128)(2,1)}, bf16[1,256,1024]...) while((s32[]{:T(128)}, ...), condition=%wide.region_6.7_spmd.clone, body=%wide.region_3.6_spmd.clone.sunk | while | flops 311458816 | bytes 39472324 | solution.py:96
  203.8 2.2 copy-done
  206.9 3.3 %fusion.45 = bf16[2,64,256]{2,1,0:T(8,128)(2,1)S(1)} fusion(bf16[2304,2,64]{0,2,1:T(8,128)(2,1)S(1)} %bitcast.105, f32[2,256]{1,0:T(2,128)S(1)} %fusion.44, f32[2,256]{1,0:T(2,128)S(1)} %get-tuple-element.204, f32[2,2304,1,256]{3,1,0,2:T(8,128)} %copy-done), kind=kOutput, calls=%fused_computation.11.clone.1 | convolution fusion | flops 154566656 | bytes 5378048 | tf_op jit(solution)/shard_map/while/body/eval_jaxpr/chsk,khd->cshd/dot_general | solution.py:90
  214.6 2.2 copy-done
  217.8 3.3 %fusion.45 = bf16[2,64,256]{2,1,0:T(8,128)(2,1)S(1)} fusion(bf16[2304,2,64]{0,2,1:T(8,128)(2,1)S(1)} %bitcast.105, f32[2,256]{1,0:T(2,128)S(1)} %fusion.44, f32[2,256]{1,0:T(2,128)S(1)} %get-tuple-element.204, f32[2,2304,1,256]{3,1,0,2:T(8,128)} %copy-done), kind=kOutput, calls=%fused_computation.11.clone.1 | convolution fusion | flops 154566656 | bytes 5378048 | tf_op jit(solution)/shard_map/while/body/eval_jaxpr/chsk,khd->cshd/dot_general | solution.py:90
  225.5 2.2 copy-done
  228.6 3.3 %fusion.45 = bf16[2,64,256]{2,1,0:T(8,128)(2,1)S(1)} fusion(bf16[2304,2,64]{0,2,1:T(8,128)(2,1)S(1)} %bitcast.105, f32[2,256]{1,0:T(2,128)S(1)} %fusion.44, f32[2,256]{1,0:T(2,128)S(1)} %get-tuple-element.204, f32[2,2304,1,256]{3,1,0,2:T(8,128)} %copy-done), kind=kOutput, calls=%fused_computation.11.clone.1 | convolution fusion | flops 154566656 | bytes 5378048 | tf_op jit(solution)/shard_map/while/body/eval_jaxpr/chsk,khd->cshd/dot_general | solution.py:90
  239.4 3.3 %fusion.45 = bf16[2,64,256]{2,1,0:T(8,128)(2,1)S(1)} fusion(bf16[2304,2,64]{0,2,1:T(8,128)(2,1)S(1)} %bitcast.105, f32[2,256]{1,0:T(2,128)S(1)} %fusion.44, f32[2,256]{1,0:T(2,128)S(1)} %get-tuple-element.204, f32[2,2304,1,256]{3,1,0,2:T(8,128)} %copy-done), kind=kOutput, calls=%fused_computation.11.clone.1 | convolution fusion | flops 154566656 | bytes 5378048 | tf_op jit(solution)/shard_map/while/body/eval_jaxpr/chsk,khd->cshd/dot_general | solution.py:90
  247.1 2.2 copy-done
  250.2 3.3 %fusion.45 = bf16[2,64,256]{2,1,0:T(8,128)(2,1)S(1)} fusion(bf16[2304,2,64]{0,2,1:T(8,128)(2,1)S(1)} %bitcast.105, f32[2,256]{1,0:T(2,128)S(1)} %fusion.44, f32[2,256]{1,0:T(2,128)S(1)} %get-tuple-element.204, f32[2,2304,1,256]{3,1,0,2:T(8,128)} %copy-done), kind=kOutput, calls=%fused_computation.11.clone.1 | convolution fusion | flops 154566656 | bytes 5378048 | tf_op jit(solution)/shard_map/while/body/eval_jaxpr/chsk,khd->cshd/dot_general | solution.py:90
  261.0 3.3 %fusion.45 = bf16[2,64,256]{2,1,0:T(8,128)(2,1)S(1)} fusion(bf16[2304,2,64]{0,2,1:T(8,128)(2,1)S(1)} %bitcast.105, f32[2,256]{1,0:T(2,128)S(1)} %fusion.44, f32[2,256]{1,0:T(2,128)S(1)} %get-tuple-element.204, f32[2,2304,1,256]{3,1,0,2:T(8,128)} %copy-done), kind=kOutput, calls=%fused_computation.11.clone.1 | convolution fusion | flops 154566656 | bytes 5378048 | tf_op jit(solution)/shard_map/while/body/eval_jaxpr/chsk,khd->cshd/dot_general | solution.py:90
  271.8 3.3 %fusion.45 = bf16[2,64,256]{2,1,0:T(8,128)(2,1)S(1)} fusion(bf16[2304,2,64]{0,2,1:T(8,128)(2,1)S(1)} %bitcast.105, f32[2,256]{1,0:T(2,128)S(1)} %fusion.44, f32[2,256]{1,0:T(2,128)S(1)} %get-tuple-element.204, f32[2,2304,1,256]{3,1,0,2:T(8,128)} %copy-done), kind=kOutput, calls=%fused_computation.11.clone.1 | convolution fusion | flops 154566656 | bytes 5378048 | tf_op jit(solution)/shard_map/while/body/eval_jaxpr/chsk,khd->cshd/dot_general | solution.py:90
  282.6 3.3 %fusion.45 = bf16[2,64,256]{2,1,0:T(8,128)(2,1)S(1)} fusion(bf16[2304,2,64]{0,2,1:T(8,128)(2,1)S(1)} %bitcast.105, f32[2,256]{1,0:T(2,128)S(1)} %fusion.44, f32[2,256]{1,0:T(2,128)S(1)} %get-tuple-element.204, f32[2,2304,1,256]{3,1,0,2:T(8,128)} %copy-done), kind=kOutput, calls=%fused_computation.11.clone.1 | convolution fusion | flops 154566656 | bytes 5378048 | tf_op jit(solution)/shard_map/while/body/eval_jaxpr/chsk,khd->cshd/dot_general | solution.py:90
  286.0 3.1 %fusion.15 = bf16[1,1,1,256,1024]{4,3,2,1,0:T(8,128)(2,1)} fusion(bf16[1024,1024]{1,0:T(8,128)(2,1)} %all-gather.5.cloned.1.call-done, bf16[1,1,1,256,1024]{4,3,2,1,0:T(8,128)(2,1)S(1)} %copy-done.2, bf16[1,256,1024]{1,2,0:T(8,128)(2,1)S(1)} %get-tuple-element.114), kind=kOutput, calls=%fused_computation.26 | convolution fusion | flops 537657344 | bytes 3670016 | tf_op jit(solution)/shard_map/dot_general | solution.py:101
  (124 shorter events, 61.6 us)
Async XLA Ops:
  6.5 74.2 %all-gather.3.cloned.1.call-start = ((), (), s32[]{:S(2)}) async-start(), calls=%async_computation | async-start | bytes 6488064 | tf_op jit(solution)/shard_map/all_gather | solution.py:39
  7.3 278.7 %all-gather.5.cloned.1.call-start = ((), (), s32[]{:S(2)}) async-start(), calls=%async_computation.1 | async-start | bytes 2162688 | tf_op jit(solution)/shard_map/all_gather | solution.py:103
  85.6 27.5 %copy-start.6 = (bf16[256,3072]{1,0:T(8,128)(2,1)}, bf16[256,3072]{1,0:T(8,128)(2,1)S(1)}, u32[]{:S(2)}) copy-start(bf16[256,3072]{1,0:T(8,128)(2,1)S(1)} %convolution_convert_fusion) | copy-start | bytes 4718596
  85.6 33.8 %copy-start.7 = (s32[1,1,1,8]{3,2,1,0:T(1,128)S(1)}, s32[1,1,1,8]{3,2,1,0:T(1,128)}, u32[]{:S(2)}) copy-start(s32[1,1,1,8]{3,2,1,0:T(1,128)} %param.11) | copy-start | bytes 100
  85.7 27.4 %copy-start.1 = (bf16[1,1,1,256,2048]{4,3,2,1,0:T(8,128)(2,1)}, bf16[1,1,1,256,2048]{4,3,2,1,0:T(8,128)(2,1)S(1)}, u32[]{:S(2)}) copy-start(bf16[1,1,1,256,2048]{4,3,2,1,0:T(8,128)(2,1)S(1)} %slice_bitcast_fusion) | copy-start | bytes 3145732
  85.7 27.4 %collective-permute-start = (bf16[1,1,1,256,2048]{4,3,2,1,0:T(8,128)(2,1)S(1)}, bf16[1,1,1,256,2048]{4,3,2,1,0:T(8,128)(2,1)S(1)}, u32[]{:S(2)}, u32[]{:S(2)}) collective-permute-start(bf16[1,1,1,256,2048]{4,3,2,1,0:T(8,128)(2,1)S(1)} %slice_bitcast_fusion), channel_id=1, source_target_pairs={{0,1},{1,2},{2,3},{3,4},{4,5},{5,6},{6,7},{7,8},{8,9},{9,10},{10,1... | collective-permute-start | bytes 3145736 | tf_op jit(solution)/shard_map/ppermute | solution.py:16
  87.9 25.2 %collective-permute-start.1 = (bf16[1,1,1,256,2048]{4,3,2,1,0:T(8,128)(2,1)S(1)}, bf16[1,1,1,256,2048]{4,3,2,1,0:T(8,128)(2,1)S(1)}, u32[]{:S(2)}, u32[]{:S(2)}) collective-permute-start(bf16[1,1,1,256,2048]{4,3,2,1,0:T(8,128)(2,1)S(1)} %slice_bitcast_fusion), channel_id=1, source_target_pairs={{1,0},{2,1},{3,2},{4,3},{5,4},{6,5},{7,6},{8,7},{9,8},{10,9},{11,1... | collective-permute-start | bytes 3145736 | tf_op jit(solution)/shard_map/ppermute | solution.py:17
  113.1 2.3 copy-start.3
  113.1 4.9 %copy-start.4 = (bf16[1,1,1,256,2048]{4,3,2,1,0:T(8,128)(2,1)}, bf16[1,1,1,256,2048]{4,3,2,1,0:T(8,128)(2,1)S(1)}, u32[]{:S(2)}) copy-start(bf16[1,1,1,256,2048]{4,3,2,1,0:T(8,128)(2,1)S(1)} %collective-permute-done.1) | copy-start | bytes 3145732
  115.4 70.2 %collective-permute-start.2 = (bf16[1,3,1,256,2048]{4,3,2,1,0:T(8,128)(2,1)}, bf16[1,3,1,256,2048]{4,3,2,1,0:T(8,128)(2,1)S(1)}, u32[]{:S(2)}, u32[]{:S(2)}) collective-permute-start(bf16[1,3,1,256,2048]{4,3,2,1,0:T(8,128)(2,1)} %pad_maximum_fusion.1), channel_id=1, source_target_pairs={{0,16},{1,17},{2,18},{3,19},{4,20},{5,21},{6,22},{7,23},{8,24},{9,... | collective-permute-start | bytes 9437192 | tf_op jit(solution)/shard_map/ppermute | solution.py:16
  118.0 71.9 %collective-permute-start.3 = (bf16[1,3,1,256,2048]{4,3,2,1,0:T(8,128)(2,1)}, bf16[1,3,1,256,2048]{4,3,2,1,0:T(8,128)(2,1)}, u32[]{:S(2)}, u32[]{:S(2)}) collective-permute-start(bf16[1,3,1,256,2048]{4,3,2,1,0:T(8,128)(2,1)} %pad_maximum_fusion.1), channel_id=1, source_target_pairs={{16,0},{17,1},{18,2},{19,3},{20,4},{21,5},{22,6},{23,7},{24,8},{25... | collective-permute-start | bytes 9437192 | tf_op jit(solution)/shard_map/ppermute | solution.py:17
  185.6 1.7 copy-start.5
  199.3 86.6 %copy-start.2 = (bf16[1,1,1,256,1024]{4,3,2,1,0:T(8,128)(2,1)S(1)}, bf16[1,1,1,256,1024]{4,3,2,1,0:T(8,128)(2,1)}, u32[]{:S(2)}) copy-start(bf16[1,1,1,256,1024]{4,3,2,1,0:T(8,128)(2,1)} %param.7) | copy-start | bytes 1572868
  203.8 2.2 copy-start
  214.6 2.2 copy-start
  225.4 2.2 copy-start
  236.3 2.2 copy-start
  247.1 2.2 copy-start
  257.9 2.2 copy-start
  268.7 2.2 copy-start
  279.5 2.2 copy-start
Sparse Core Ops, SparseCore 0:
  10.2 70.4 all-gather.2
  119.5 60.8 all-gather.4
where the time goes:
time: 297 us; the launch traced here: 296 us
  waiting for transfers between devices  160 us (54%)
  local copies, waits for them, and re-layouts  49.5 us (17%)
  matrix products  47.9 us (16%)
  other arithmetic  14.6 us (5%)
  between operations  13.6 us (5%)
  starting transfers between devices  9.55 us (3%)
    ppermute x2, waiting for transfers between devices, padded(): before = lax.ppermute(last, axis, up)  86 us
    all_gather x1, waiting for transfers between devices, shards(): lax.all_gather(qkv_weight, ('region', 'owner'), axis=0, tiled=True)  70.9 us
    dot_general x8, matrix products, attend_group(): jnp.einsum('chsk,khd->cshd', attn_probs, value_part, preferred_element_ty...  26.1 us
    while x16, local copies, waits for them, and re-layouts  17.8 us
    dot_general x8, matrix products, attend_group(): jnp.einsum('cshd,khd->chsk', query_part, key_part, preferred_element_type...  13.9 us
    dynamic_slice x16, local copies, waits for them, and re-layouts, attend_group(): lax.dynamic_slice_in_dim(key_rows, offset, group_cols, 1)  12.8 us
    dynamic_slice x16, local copies, waits for them, and re-layouts, attend_group(): lax.dynamic_slice_in_dim(queries, offset, group_cols, 2)  7.67 us
    concatenate x2, other arithmetic, padded(): value = jnp.concatenate([before, value, after], axis=dim)  6.92 us
  transfers between devices with their start and end apart: 6, of which 4 were waited for; matrix products, arithmetic and copies ran while one was open for 28% of the time, Pallas kernels for 0%

commit v1 on v0

v1 whole, which is shorter than its diff:
```python
import functools

import jax
import jax.numpy as jnp
from jax import lax
from jax.experimental import pallas as pl
from jax.experimental.pallas import tpu as pltpu
from jax.sharding import PartitionSpec as P

HEAD_DIM = 64
MESH = pl.DeviceIdType.MESH
SIB, UP, DOWN, ACROSS, REGION = range(5)


def padded(value, sides, width):
    for axis, dim in sides:
        devices, length = (lax.axis_size(axis), value.shape[dim])
        up = [(i, (i + 1) % devices) for i in range(devices - 1)]
        down = [(j, i) for i, j in up]
        last = lax.slice_in_dim(value, length - width, length, axis=dim)
        first = lax.slice_in_dim(value, 0, width, axis=dim)
        before = lax.ppermute(last, axis, up)
        after = lax.ppermute(first, axis, down)
        value = jnp.concatenate([before, value, after], axis=dim)
    return value


def exchange_kernel(owners, x_ref, wq_ref, wo_ref, xs_ref, gq_ref, go_ref,
                    send_q, recv_q, send_o, recv_o, send_x, recv_x, local_sem):
    planes = owners // 4
    region = lax.axis_index("region")
    owner = lax.axis_index("owner")
    core = lax.rem(owner, 2)
    row = lax.rem(owner // 2, 2)
    plane = owner // 4
    side_owner = owner + 2 * core - 1
    has_side = jnp.logical_and(side_owner >= 0, side_owner < owners)
    has_up = plane < planes - 1
    has_down = plane > 0

    def owner_of(z, y, c):
        return z * 4 + y * 2 + c

    targets = {
        SIB: (region, owner_of(plane, row, 1 - core)),
        UP: (region, owner_of(plane + 1, row, core)),
        DOWN: (region, owner_of(plane - 1, row, core)),
        ACROSS: (region, owner_of(plane, 1 - row, core)),
        REGION: (1 - region, owner),
    }
    conditions = {SIB: None, UP: has_up, DOWN: has_down, ACROSS: None, REGION: None}
    side = (region, side_owner)

    barrier = pltpu.get_barrier_semaphore()
    for kind, target in targets.items():
        def greet(target=target):
            pl.semaphore_signal(barrier, inc=1, device_id=target, device_id_type=MESH)
        if conditions[kind] is None:
            greet()
        else:
            pl.when(conditions[kind])(greet)

    @pl.when(has_side)
    def _():
        pl.semaphore_signal(barrier, inc=1, device_id=side, device_id_type=MESH)

    pl.semaphore_wait(
        barrier,
        3 + has_up.astype(jnp.int32) + has_down.astype(jnp.int32) + has_side.astype(jnp.int32),
    )

    pending = []

    def run(cond, fn):
        if cond is None:
            fn()
        else:
            pl.when(cond)(fn)

    def both(a, b):
        if a is None:
            return b
        return a if b is None else jnp.logical_and(a, b)

    def start(cond, make):
        run(cond, lambda: make().start())
        pending.append((cond, lambda: make().wait_send()))

    weights = {
        "q": (wq_ref, gq_ref, send_q, recv_q),
        "o": (wo_ref, go_ref, send_o, recv_o),
    }

    def rows_of(ref, shard, src):
        depth = shard.shape[0]
        return ref.at[pl.ds(pl.multiple_of(src * depth, depth), depth), :]

    def send(name, kind, src, cond, own=False):
        shard, full, send_sem, recv_sem = weights[name]
        cond = both(cond, conditions[kind])

        def make():
            return pltpu.make_async_remote_copy(
                src_ref=shard if own else rows_of(full, shard, src),
                dst_ref=rows_of(full, shard, src),
                send_sem=send_sem.at[kind, src],
                recv_sem=recv_sem.at[src],
                device_id=targets[kind],
                device_id_type=MESH,
            )

        start(cond, make)

    def arrive(name, src, cond):
        shard, full, send_sem, recv_sem = weights[name]

        def wait():
            pltpu.make_async_remote_copy(
                src_ref=rows_of(full, shard, src),
                dst_ref=rows_of(full, shard, src),
                send_sem=send_sem.at[SIB, src],
                recv_sem=recv_sem.at[src],
                device_id=targets[SIB],
                device_id_type=MESH,
            ).wait_recv()

        run(cond, wait)

    def send_block(src_ref, slot, target, sem, cond):
        def make():
            return pltpu.make_async_remote_copy(
                src_ref=src_ref,
                dst_ref=xs_ref.at[slot],
                send_sem=send_x.at[sem],
                recv_sem=recv_x.at[slot],
                device_id=target,
                device_id_type=MESH,
            )

        start(cond, make)

    def arrive_block(slot, cond):
        def wait():
            pltpu.make_async_remote_copy(
                src_ref=xs_ref.at[slot],
                dst_ref=xs_ref.at[slot],
                send_sem=send_x.at[0],
                recv_sem=recv_x.at[slot],
                device_id=targets[SIB],
                device_id_type=MESH,
            ).wait_recv()

        run(cond, wait)

    def ident(r, z, y, c):
        return r * owners + owner_of(z, y, c)

    me = ident(region, plane, row, core)
    for kind in (UP, DOWN, ACROSS):
        send("q", kind, me, None, own=True)
    send_block(x_ref, 4, targets[REGION], 0, None)
    send("q", REGION, me, None, own=True)
    send("o", ACROSS, me, None, own=True)
    send_block(x_ref, 1 - core, side, 1, has_side)
    send("q", SIB, me, None, own=True)
    send("o", SIB, me, None, own=True)
    send_block(x_ref, core, targets[SIB], 2, None)
    local_q = pltpu.make_async_copy(wq_ref, rows_of(gq_ref, wq_ref, me), local_sem.at[0])
    local_o = pltpu.make_async_copy(wo_ref, rows_of(go_ref, wo_ref, me), local_sem.at[1])
    local_q.start()
    local_o.start()

    def at_distance(d):
        if d == 0:
            return [(plane, None, ())]
        return [
            (plane - d, plane - d >= 0, (UP,)),
            (plane + d, plane + d < planes, (DOWN,)),
        ]

    def row_step(d):
        for z, cond, _ in at_distance(d):
            src = ident(region, z, 1 - row, core)
            arrive("q", src, cond)
            send("q", REGION, src, cond)
            send("q", SIB, src, cond)

    def plane_step(d):
        for z, cond, onward in at_distance(d):
            src = ident(region, z, row, core)
            arrive("q", src, cond)
            for kind in onward + (ACROSS, REGION, SIB):
                send("q", kind, src, cond)

    row_step(0)
    for d in range(1, planes):
        plane_step(d)
        row_step(d)
        if d == 1:
            arrive_block(4, None)
            send_block(xs_ref.at[4], 2 + core, targets[SIB], 3, None)
            send_block(xs_ref.at[4], 3 - core, side, 4, has_side)

    send("o", REGION, me, None, own=True)
    for kind in (UP, DOWN):
        send("o", kind, me, None, own=True)
    src = ident(region, plane, 1 - row, core)
    arrive("o", src, None)
    for kind in (REGION, UP, DOWN, SIB):
        send("o", kind, src, None)
    for y in (row, 1 - row):
        src = ident(1 - region, plane, y, core)
        arrive("o", src, None)
        for kind in (UP, DOWN, SIB):
            send("o", kind, src, None)
    def region_q(d):
        order = [row, 1 - row] if d == 0 else [row, 1 - row]
        for y in order:
            for z, cond, _ in at_distance(d):
                src = ident(1 - region, z, y, core)
                arrive("q", src, cond)
                send("q", SIB, src, cond)

    def plane_o(d):
        for r, y in ((region, row), (region, 1 - row), (1 - region, row), (1 - region, 1 - row)):
            for z, cond, onward in at_distance(d):
                src = ident(r, z, y, core)
                arrive("o", src, cond)
                for kind in onward + (SIB,):
                    send("o", kind, src, cond)

    region_q(0)
    for d in range(1, planes):
        region_q(d)
        plane_o(d)

    for name in ("q", "o"):
        for d in range(planes):
            for r in (region, 1 - region):
                for y in (row, 1 - row):
                    for z, cond, _ in at_distance(d):
                        arrive(name, ident(r, z, y, 1 - core), cond)
    arrive_block(1 - core, None)
    arrive_block(3 - core, None)
    arrive_block(core, has_side)
    arrive_block(2 + core, has_side)
    for cond, wait in pending:
        run(cond, wait)
    local_q.wait()
    local_o.wait()


def exchange(block, qkv_weight, out_weight):
    owners = lax.axis_size("owner")
    devices = lax.axis_size("region") * owners
    anywhere = pl.BlockSpec(memory_space=pl.ANY)
    return pl.pallas_call(
        functools.partial(exchange_kernel, owners),
        out_shape=[
            jax.ShapeDtypeStruct((5,) + block.shape, block.dtype),
            jax.ShapeDtypeStruct((devices * qkv_weight.shape[0], qkv_weight.shape[1]), qkv_weight.dtype),
            jax.ShapeDtypeStruct((devices * out_weight.shape[0], out_weight.shape[1]), out_weight.dtype),
        ],
        in_specs=[anywhere] * 3,
        out_specs=[anywhere] * 3,
        scratch_shapes=[
            pltpu.SemaphoreType.DMA((5, devices)),
            pltpu.SemaphoreType.DMA((devices,)),
            pltpu.SemaphoreType.DMA((5, devices)),
            pltpu.SemaphoreType.DMA((devices,)),
            pltpu.SemaphoreType.DMA((5,)),
            pltpu.SemaphoreType.DMA((5,)),
            pltpu.SemaphoreType.DMA((2,)),
        ],
        compiler_params=pltpu.CompilerParams(collective_id=0, has_side_effects=True),
        name="exchange",
    )(block, qkv_weight, out_weight)


def layer_norm(inputs, norm_gain):
    widened = inputs.astype(jnp.float32)
    average = jnp.mean(widened, axis=-1, keepdims=True)
    spread = jnp.mean((widened - average) ** 2, axis=-1, keepdims=True)
    return ((widened - average) * lax.rsqrt(spread + 1e-06) * norm_gain).astype(jnp.bfloat16)


def attend_kernel(listed_ref, x_ref, xs_ref, gain_ref, bias_ref, wq_ref, wo_ref, out_ref,
                  normed_ref, q_ref, kv_ref, mixed_ref):
    tokens, width = x_ref.shape
    others = xs_ref.shape[0]
    gain = gain_ref[...]
    normed_ref[0:tokens, :] = layer_norm(x_ref[...], gain)

    @pl.loop(0, others)
    def _(slot):
        rows = pl.ds(pl.multiple_of((slot + 1) * tokens, tokens), tokens)
        block = xs_ref[slot].astype(jnp.float32)
        block = jnp.where(listed_ref[slot] > 0, block, 0.0)
        normed_ref[rows, :] = layer_norm(block, gain)

    tile = min(512, width)

    @pl.loop(0, width // tile)
    def _(step):
        cols = pl.ds(pl.multiple_of(step * tile, tile), tile)
        part = jnp.dot(normed_ref[0:tokens, :], wq_ref[:, cols], preferred_element_type=jnp.float32)
        q_ref[:, cols] = part.astype(jnp.bfloat16) * jnp.bfloat16(HEAD_DIM ** (-0.5))

    @pl.loop(0, 2 * width // tile)
    def _(step):
        cols = pl.ds(pl.multiple_of(step * tile, tile), tile)
        from_cols = pl.ds(pl.multiple_of(width + step * tile, tile), tile)
        kv_ref[:, cols] = jnp.dot(
            normed_ref[...], wq_ref[:, from_cols], preferred_element_type=jnp.float32
        ).astype(jnp.bfloat16)

    pair = 2 * HEAD_DIM
    low = lax.broadcasted_iota(jnp.int32, (tokens, pair), 1) < HEAD_DIM
    bias = bias_ref[...]

    @pl.loop(0, width // pair)
    def _(group):
        cols = pl.ds(pl.multiple_of(group * pair, pair), pair)
        value_cols = pl.ds(pl.multiple_of(width + group * pair, pair), pair)
        queries = q_ref[:, cols]
        keys = kv_ref[:, cols]
        values = kv_ref[:, value_cols]
        halves = []
        for mine in (low, jnp.logical_not(low)):
            query = jnp.where(mine, queries, jnp.zeros_like(queries))
            scores = lax.dot_general(
                query, keys, (((1,), (1,)), ((), ())), preferred_element_type=jnp.float32
            ) + bias
            shifted = jnp.exp(scores - jnp.max(scores, axis=-1, keepdims=True))
            total = jnp.sum(shifted, axis=-1, keepdims=True)
            mixed = jnp.dot(shifted.astype(jnp.bfloat16), values, preferred_element_type=jnp.float32)
            halves.append(mixed / total)
        mixed_ref[:, cols] = jnp.where(low, halves[0], halves[1]).astype(jnp.bfloat16)

    @pl.loop(0, width // tile)
    def _(step):
        cols = pl.ds(pl.multiple_of(step * tile, tile), tile)
        projected = jnp.dot(mixed_ref[...], wo_ref[:, cols], preferred_element_type=jnp.float32)
        out_ref[:, cols] = (x_ref[:, cols].astype(jnp.float32) + projected).astype(out_ref.dtype)


def attend(listed, block, others, norm_gain, bias, qkv_weight, out_weight):
    tokens, width = block.shape
    count = (others.shape[0] + 1) * tokens
    vmem = pl.BlockSpec(memory_space=pltpu.VMEM)
    return pl.pallas_call(
        attend_kernel,
        out_shape=jax.ShapeDtypeStruct(block.shape, block.dtype),
        in_specs=[pl.BlockSpec(memory_space=pltpu.SMEM)] + [vmem] * 6,
        out_specs=vmem,
        scratch_shapes=[
            pltpu.VMEM((count, width), jnp.bfloat16),
            pltpu.VMEM((tokens, width), jnp.bfloat16),
            pltpu.VMEM((count, 2 * width), jnp.bfloat16),
            pltpu.VMEM((tokens, width), jnp.bfloat16),
        ],
        compiler_params=pltpu.CompilerParams(vmem_limit_bytes=60 * 1024 * 1024),
        name="attend",
    )(listed, block, others, norm_gain, bias, qkv_weight, out_weight)


def shards(voxels, norm_gain, qkv_weight, out_weight, neighbours):
    block_size, model_width = voxels.shape[-2:]
    block = voxels.reshape(block_size, model_width)
    regions, owners = (lax.axis_size("region"), lax.axis_size("owner"))
    region, owner = (lax.axis_index("region"), lax.axis_index("owner"))
    if regions == 2 and owners % 4 == 0 and owners > 4:
        others, full_qkv, full_out = exchange(block, qkv_weight, out_weight)
        offsets = [(0, -1), (0, 1), (1 - 2 * region, -1), (1 - 2 * region, 1), (1 - 2 * region, 0)]
    else:
        wide = padded(voxels[:, :, 0], (("owner", 1), ("region", 0)), 1)
        wide = wide.reshape(-1, block_size, model_width)
        middle = wide.shape[0] // 2
        others = jnp.concatenate([wide[:middle], wide[middle + 1:]], axis=0)
        full_qkv = lax.all_gather(qkv_weight, ("region", "owner"), axis=0, tiled=True)
        full_out = lax.all_gather(out_weight, ("region", "owner"), axis=0, tiled=True)
        offsets = [(i, j) for i in (-1, 0, 1) for j in (-1, 0, 1) if i or j]
    numbers = []
    for up, along in offsets:
        inside = (owner + along >= 0) & (owner + along < owners)
        number = (region + up) * owners + owner + along
        numbers.append(jnp.where(inside & (number >= 0), number, -2))
    listed = jnp.any(neighbours.reshape(1, -1) == jnp.stack(numbers)[:, None], axis=1)
    present = jnp.concatenate([jnp.ones((1,), bool), listed])
    bias = jnp.repeat(jnp.where(present, 0.0, -1e30).astype(jnp.float32), block_size)[None, :]
    out = attend(
        listed.astype(jnp.int32), block, others, norm_gain[None, :], bias, full_qkv, full_out
    )
    return out.reshape(voxels.shape)


def solution(mesh):
    return jax.shard_map(
        shards,
        mesh=mesh,
        in_specs=(
            P("region", "owner", None, None, None),
            P(),
            P(("region", "owner"), None),
            P(("region", "owner"), None),
            P("region", "owner", None, None),
        ),
        out_specs=P("region", "owner", None, None, None),
        check_vma=False,
    )
```

time: 297 us -> 107 us (0.36)
  waiting for transfers between devices: 160 us -> 0 us
  Pallas kernels: 0 us -> 104 us
  local copies, waits for them, and re-layouts: 49.5 us -> 0.75 us
  matrix products: 47.9 us -> 0 us
  between operations: 13.6 us -> 0.01 us
  other arithmetic: 14.6 us -> 1.44 us
  starting transfers between devices: 9.55 us -> 0 us
    pallas_call x0 -> x2, Pallas kernels: none -> 104 us  [the longest x1 74.7 us: exchange(): pl.pallas_call(functools.partial(exchange_kernel, owners), out_shape=[jax...]
    ppermute x4 -> x0, waiting for transfers between devices: 88.6 us -> none  [the longest x2 86 us: padded(): before = lax.ppermute(last, axis, up)]
    all_gather x2 -> x0, waiting for transfers between devices: 70.9 us -> none  [the longest x1 70.9 us: shards(): lax.all_gather(qkv_weight, ('region', 'owner'), axis=0, tiled=True)]
    dot_general x18 -> x0, matrix products: 47.9 us -> none  [the longest x8 26.1 us: attend_group(): jnp.einsum('chsk,khd->cshd', attn_probs, value_part, preferred_element_ty...]
    dynamic_slice x40 -> x0, local copies, waits for them, and re-layouts: 22.4 us -> none  [the longest x16 12.8 us: attend_group(): lax.dynamic_slice_in_dim(key_rows, offset, group_cols, 1)]
    while x16 -> x0, local copies, waits for them, and re-layouts: 17.8 us -> none
    ppermute x4 -> x0, starting transfers between devices: 9.51 us -> none  [the longest x2 4.81 us: padded(): before = lax.ppermute(last, axis, up)]
    reduce_sum x10 -> x0, other arithmetic: 7.58 us -> none  [the longest x8 5.07 us: attend_group(): jnp.sum(shifted, axis=-1, keepdims=True)]
  transfers between devices with their start and end apart: 6 -> 0, of which waited for: 4 -> 0; matrix products, arithmetic and copies ran while one was open for 28% -> 0% of each run, Pallas kernels for 0% -> 0%
where the time goes in v1:
time: 107 us; the launch traced here: 106 us
  Pallas kernels  104 us (97%)
  other arithmetic  1.44 us (1%)
    pallas_call x1, Pallas kernels, exchange(): pl.pallas_call(functools.partial(exchange_kernel, owners), out_shape=[jax...  74.7 us
    pallas_call x1, Pallas kernels, attend(): pl.pallas_call(attend_kernel, out_shape=jax.ShapeDtypeStruct(block.shape,...  29 us

profile of v1, /device:TPU:4, one launch (start us, length us, event | category | flops | bytes accessed | tf_op | source)
XLA Modules:
  0.0 106.0 jit_solution(1265041509755519239)
XLA Ops:
  0.0 0.1 stack.23
  0.1 0.8 compare_reduce_fusion
  0.9 0.1 add_select_fusion
  1.0 0.5 convert_element_type.3.listed_ref
  1.5 0.1 broadcast_bitcast_fusion
  1.6 0.6 copy.6
  2.2 74.7 %exchange.1 = (bf16[5,256,1024]{2,1,0:T(8,128)(2,1)}, bf16[1024,3072]{1,0:T(8,128)(2,1)}, bf16[1024,1024]{1,0:T(8,128)(2,1)}) custom-call(bf16[256,1024]{1,0:T(8,128)(2,1)} %bitcast.13, bf16[32,3072]{1,0:T(8,128)(2,1)} %wq_ref.1, bf16[32,1024]{1,0:T(8,128)(2,1)} %wo_ref.1), custom_call_target="tpu_custom_call" | custom-call | tf_op jit(solution)/shard_map/exchange/pallas_call | solution.py:257
  76.9 29.0 %attend.1 = bf16[256,1024]{1,0:T(8,128)(2,1)} custom-call(s32[5]{0:T(128)} %convert_element_type.3.listed_ref, bf16[256,1024]{1,0:T(8,128)(2,1)} %bitcast.14, bf16[5,256,1024]{2,1,0:T(8,128)(2,1)} %get-tuple-element.8.xs_ref, f32[1,1024]{1,0:T(1,128)} %bitcast.16, f32[1,1536]{1,0:T(1,128)} %bitcast.15, bf16[1024,3072]{1,0:T(8,128)(2,1)} %get-tuple-element.9.wq_ref, ...), custom_call_target="tpu_custom_call" | custom-call | tf_op jit(solution)/shard_map/attend/pallas_call | solution.py:351

commit v2 on v1

v2 whole, which is shorter than its diff:
```python
import functools

import jax
import jax.numpy as jnp
from jax import lax
from jax.experimental import pallas as pl
from jax.experimental.pallas import tpu as pltpu
from jax.sharding import PartitionSpec as P

HEAD_DIM = 64
MESH = pl.DeviceIdType.MESH
GROUPS = 4
SIB, UP, DOWN, ACROSS, REGION = range(5)


def padded(value, sides, width):
    for axis, dim in sides:
        devices, length = (lax.axis_size(axis), value.shape[dim])
        up = [(i, (i + 1) % devices) for i in range(devices - 1)]
        down = [(j, i) for i, j in up]
        last = lax.slice_in_dim(value, length - width, length, axis=dim)
        first = lax.slice_in_dim(value, 0, width, axis=dim)
        before = lax.ppermute(last, axis, up)
        after = lax.ppermute(first, axis, down)
        value = jnp.concatenate([before, value, after], axis=dim)
    return value


def layer_norm(inputs, norm_gain):
    widened = inputs.astype(jnp.float32)
    average = jnp.mean(widened, axis=-1, keepdims=True)
    spread = jnp.mean((widened - average) ** 2, axis=-1, keepdims=True)
    return ((widened - average) * lax.rsqrt(spread + 1e-06) * norm_gain).astype(jnp.bfloat16)


def attend_heads(queries, keys, values, bias):
    tokens, pair = queries.shape
    low = lax.broadcasted_iota(jnp.int32, (tokens, pair), 1) < HEAD_DIM
    halves = []
    for mine in (low, jnp.logical_not(low)):
        query = jnp.where(mine, queries, jnp.zeros_like(queries))
        scores = lax.dot_general(
            query, keys, (((1,), (1,)), ((), ())), preferred_element_type=jnp.float32
        ) + bias
        shifted = jnp.exp(scores - jnp.max(scores, axis=-1, keepdims=True))
        total = jnp.sum(shifted, axis=-1, keepdims=True)
        mixed = jnp.dot(shifted.astype(jnp.bfloat16), values, preferred_element_type=jnp.float32)
        halves.append(mixed / total)
    return jnp.where(low, halves[0], halves[1]).astype(jnp.bfloat16)


def fused_kernel(owners, x_ref, wq_ref, wo_ref, gain_ref, bias_ref, out_ref,
                 xs_ref, gq_ref, go_ref, normed_ref, q_ref, kv_ref, mixed_ref,
                 send_q, recv_q, send_o, recv_o, send_x, recv_x, local_sem):
    groups = wq_ref.shape[0]
    share = wq_ref.shape[2] // 3
    tokens, width = x_ref.shape
    others = xs_ref.shape[0]
    planes = owners // 4
    region = lax.axis_index("region")
    owner = lax.axis_index("owner")
    core = lax.rem(owner, 2)
    row = lax.rem(owner // 2, 2)
    plane = owner // 4
    side_owner = owner + 2 * core - 1
    has_side = jnp.logical_and(side_owner >= 0, side_owner < owners)
    has_up = plane < planes - 1
    has_down = plane > 0

    def owner_of(z, y, c):
        return z * 4 + y * 2 + c

    def ident(r, z, y, c):
        return r * owners + owner_of(z, y, c)

    targets = {
        SIB: (region, owner_of(plane, row, 1 - core)),
        UP: (region, owner_of(plane + 1, row, core)),
        DOWN: (region, owner_of(plane - 1, row, core)),
        ACROSS: (region, owner_of(plane, 1 - row, core)),
        REGION: (1 - region, owner),
    }
    conditions = {SIB: None, UP: has_up, DOWN: has_down, ACROSS: None, REGION: None}
    side = (region, side_owner)

    def run(cond, fn):
        if cond is None:
            fn()
        else:
            pl.when(cond)(fn)

    def both(a, b):
        if a is None:
            return b
        return a if b is None else jnp.logical_and(a, b)

    barrier = pltpu.get_barrier_semaphore()

    def greet(target):
        pl.semaphore_signal(barrier, inc=1, device_id=target, device_id_type=MESH)

    for kind, target in targets.items():
        run(conditions[kind], functools.partial(greet, target))
    run(has_side, functools.partial(greet, side))
    pl.semaphore_wait(
        barrier,
        3 + has_up.astype(jnp.int32) + has_down.astype(jnp.int32) + has_side.astype(jnp.int32),
    )

    pending = []

    def start(cond, make):
        run(cond, lambda: make().start())
        pending.append((cond, lambda: make().wait_send()))

    def whole(name):
        return go_ref if name == "o" else gq_ref.at[name]

    def own_shard(name):
        return wo_ref if name == "o" else wq_ref.at[name]

    def rows_of(name, src):
        depth = wo_ref.shape[0]
        return whole(name).at[pl.ds(pl.multiple_of(src * depth, depth), depth), :]

    def send_sem(name, kind, src):
        return send_o.at[kind, src // 2] if name == "o" else send_q.at[name, kind, src // 2]

    def recv_sem(name, src):
        return recv_o.at[src] if name == "o" else recv_q.at[name, src]

    def send(name, kind, src, cond, own=False):
        def make():
            return pltpu.make_async_remote_copy(
                src_ref=own_shard(name) if own else rows_of(name, src),
                dst_ref=rows_of(name, src),
                send_sem=send_sem(name, kind, src),
                recv_sem=recv_sem(name, src),
                device_id=targets[kind],
                device_id_type=MESH,
            )

        start(both(cond, conditions[kind]), make)

    def arrive(name, src, cond):
        def wait():
            pltpu.make_async_remote_copy(
                src_ref=rows_of(name, src),
                dst_ref=rows_of(name, src),
                send_sem=send_sem(name, SIB, src),
                recv_sem=recv_sem(name, src),
                device_id=targets[SIB],
                device_id_type=MESH,
            ).wait_recv()

        run(cond, wait)

    def block_copy(src_ref, slot, target, sem):
        return pltpu.make_async_remote_copy(
            src_ref=src_ref,
            dst_ref=xs_ref.at[slot],
            send_sem=send_x.at[sem],
            recv_sem=recv_x.at[slot],
            device_id=target,
            device_id_type=MESH,
        )

    def send_block(src_ref, slot, target, sem, cond):
        start(cond, lambda: block_copy(src_ref, slot, target, sem))

    def arrive_block(slot, cond):
        run(cond, lambda: block_copy(xs_ref.at[slot], slot, targets[SIB], 0).wait_recv())

    me = ident(region, plane, row, core)

    def at_distance(d):
        if d == 0:
            return [(plane, None, ())]
        return [
            (plane - d, plane - d >= 0, (UP,)),
            (plane + d, plane + d < planes, (DOWN,)),
        ]

    def row_step(g, d):
        for z, cond, _ in at_distance(d):
            src = ident(region, z, 1 - row, core)
            arrive(g, src, cond)
            send(g, REGION, src, cond)
            send(g, SIB, src, cond)

    def plane_step(g, d):
        for z, cond, onward in at_distance(d):
            src = ident(region, z, row, core)
            arrive(g, src, cond)
            for kind in onward + (ACROSS, REGION, SIB):
                send(g, kind, src, cond)

    def own_step(g):
        for kind in (UP, DOWN, ACROSS, REGION, SIB):
            send(g, kind, me, None, own=True)

    def region_step(g, d):
        for y in (row, 1 - row):
            for z, cond, _ in at_distance(d):
                src = ident(1 - region, z, y, core)
                arrive(g, src, cond)
                send(g, SIB, src, cond)

    def sibling_step(name):
        for d in range(planes):
            for r in (region, 1 - region):
                for y in (row, 1 - row):
                    for z, cond, _ in at_distance(d):
                        arrive(name, ident(r, z, y, 1 - core), cond)

    def near_steps(g, own=True):
        steps = [functools.partial(own_step, g)] if own else []
        steps.append(functools.partial(row_step, g, 0))
        for d in range(1, planes):
            steps.append(functools.partial(plane_step, g, d))
            steps.append(functools.partial(row_step, g, d))
        return steps

    def far_steps(g):
        steps = [functools.partial(region_step, g, d) for d in range(planes)]
        return steps + [functools.partial(sibling_step, g)]

    def out_across():
        src = ident(region, plane, 1 - row, core)
        arrive("o", src, None)
        for kind in (REGION, UP, DOWN, SIB):
            send("o", kind, src, None)

    def out_region():
        for y in (row, 1 - row):
            src = ident(1 - region, plane, y, core)
            arrive("o", src, None)
            for kind in (UP, DOWN, SIB):
                send("o", kind, src, None)

    def out_plane(d):
        for r, y in ((region, row), (region, 1 - row), (1 - region, row), (1 - region, 1 - row)):
            for z, cond, onward in at_distance(d):
                src = ident(r, z, y, core)
                arrive("o", src, cond)
                for kind in onward + (SIB,):
                    send("o", kind, src, cond)

    def out_own():
        for kind in (ACROSS, REGION, UP, DOWN, SIB):
            send("o", kind, me, None, own=True)

    gain = gain_ref[...]

    def norm_block(slot):
        rows = pl.ds(pl.multiple_of((slot + 1) * tokens, tokens), tokens)
        normed_ref[rows, :] = layer_norm(xs_ref[slot], gain)

    bias = bias_ref[...]
    pair = 2 * HEAD_DIM

    def project(g, first, rows):
        kv_ref[first:first + rows, :] = jnp.dot(
            normed_ref[first:first + rows, :], gq_ref[g, :, share:],
            preferred_element_type=jnp.float32,
        ).astype(jnp.bfloat16)

    def project_queries(g):
        part = jnp.dot(
            normed_ref[0:tokens, :], gq_ref[g, :, 0:share], preferred_element_type=jnp.float32
        )
        q_ref[...] = part.astype(jnp.bfloat16) * jnp.bfloat16(HEAD_DIM ** (-0.5))

    def attend_pair(g, at):
        mixed_ref[:, g * share + at:g * share + at + pair] = attend_heads(
            q_ref[:, at:at + pair],
            kv_ref[:, at:at + pair],
            kv_ref[:, share + at:share + at + pair],
            bias,
        )

    def compute_steps(g):
        count = (others + 1) * tokens
        steps = [functools.partial(project_queries, g)]
        steps += [functools.partial(project, g, i, tokens) for i in range(0, count, tokens)]
        return steps + [functools.partial(attend_pair, g, at) for at in range(0, share, pair)]

    def interleave(work, steps):
        done = 0
        for i, piece in enumerate(work):
            piece()
            due = (i + 1) * len(steps) // len(work)
            for step in steps[done:due]:
                step()
            done = due

    for kind in (UP, DOWN, ACROSS):
        send(0, kind, me, None, own=True)
    send_block(x_ref, 4, targets[REGION], 0, None)
    for kind in (REGION, SIB):
        send(0, kind, me, None, own=True)
    send_block(x_ref, 1 - core, side, 1, has_side)
    send_block(x_ref, core, targets[SIB], 2, None)
    local = [
        pltpu.make_async_copy(own_shard(name), rows_of(name, me), local_sem.at[i])
        for i, name in enumerate(list(range(groups)) + ["o"])
    ]
    for copy in local:
        copy.start()

    @pl.when(jnp.logical_not(has_side))
    def _():
        xs_ref[core] = jnp.zeros((tokens, width), xs_ref.dtype)
        xs_ref[2 + core] = jnp.zeros((tokens, width), xs_ref.dtype)

    normed_ref[0:tokens, :] = layer_norm(x_ref[...], gain)

    def relay():
        arrive_block(4, None)
        send_block(xs_ref.at[4], 2 + core, targets[SIB], 3, None)
        send_block(xs_ref.at[4], 3 - core, side, 4, has_side)

    def norm_step(slot, cond, wait=True):
        if wait:
            arrive_block(slot, cond)
        norm_block(slot)

    first = near_steps(0, own=False)
    for step in first[:3] + [relay] + first[3:]:
        step()
    norms = [
        functools.partial(norm_step, 1 - core, None),
        functools.partial(norm_step, 4, None, False),
        functools.partial(norm_step, core, has_side),
        functools.partial(norm_step, 3 - core, None),
        functools.partial(norm_step, 2 + core, has_side),
    ]
    interleave(norms, near_steps(1))
    for copy in local:
        copy.wait()
    for step in far_steps(0):
        step()
    out_steps = [out_own, out_across, out_region] + [
        functools.partial(out_plane, d) for d in range(1, planes)
    ] + [functools.partial(sibling_step, "o")]
    half = len(out_steps) // 2
    for g in range(groups):
        steps = []
        if g + 2 < groups:
            steps += near_steps(g + 2)
        if g + 2 == groups:
            steps += out_steps[:half]
        if g + 1 < groups:
            steps += far_steps(g + 1)
        if g + 1 == groups:
            steps += out_steps[half:]
        interleave(compute_steps(g), steps)

    tile = min(512, width)
    for at in range(0, width, tile):
        projected = jnp.dot(
            mixed_ref[...], go_ref[:, at:at + tile], preferred_element_type=jnp.float32
        )
        out_ref[:, at:at + tile] = (
            x_ref[:, at:at + tile].astype(jnp.float32) + projected
        ).astype(out_ref.dtype)
    for cond, wait in pending:
        run(cond, wait)


def fused(block, qkv_weight, out_weight, norm_gain, bias):
    owners = lax.axis_size("owner")
    devices = lax.axis_size("region") * owners
    tokens, width = block.shape
    depth = qkv_weight.shape[0]
    groups = GROUPS
    share = width // groups
    parted = qkv_weight.reshape(depth, 3, groups, share).transpose(2, 0, 1, 3)
    parted = parted.reshape(groups, depth, 3 * share)
    count = bias.shape[1]
    vmem = pl.BlockSpec(memory_space=pltpu.VMEM)
    return pl.pallas_call(
        functools.partial(fused_kernel, owners),
        out_shape=jax.ShapeDtypeStruct(block.shape, block.dtype),
        in_specs=[vmem] * 5,
        out_specs=vmem,
        scratch_shapes=[
            pltpu.VMEM((5, tokens, width), block.dtype),
            pltpu.VMEM((groups, devices * depth, 3 * share), qkv_weight.dtype),
            pltpu.VMEM((devices * depth, width), out_weight.dtype),
            pltpu.VMEM((count, width), jnp.bfloat16),
            pltpu.VMEM((tokens, share), jnp.bfloat16),
            pltpu.VMEM((count, 2 * share), jnp.bfloat16),
            pltpu.VMEM((tokens, width), jnp.bfloat16),
            pltpu.SemaphoreType.DMA((groups, 5, devices // 2)),
            pltpu.SemaphoreType.DMA((groups, devices)),
            pltpu.SemaphoreType.DMA((5, devices // 2)),
            pltpu.SemaphoreType.DMA((devices,)),
            pltpu.SemaphoreType.DMA((5,)),
            pltpu.SemaphoreType.DMA((5,)),
            pltpu.SemaphoreType.DMA((groups + 1,)),
        ],
        compiler_params=pltpu.CompilerParams(
            collective_id=0, has_side_effects=True, vmem_limit_bytes=60 * 1024 * 1024
        ),
        name="fused",
    )(block, parted, out_weight, norm_gain, bias)


def attend_kernel(listed_ref, x_ref, xs_ref, gain_ref, bias_ref, wq_ref, wo_ref, out_ref,
                  normed_ref, q_ref, kv_ref, mixed_ref):
    tokens, width = x_ref.shape
    others = xs_ref.shape[0]
    gain = gain_ref[...]
    normed_ref[0:tokens, :] = layer_norm(x_ref[...], gain)

    @pl.loop(0, others)
    def _(slot):
        rows = pl.ds(pl.multiple_of((slot + 1) * tokens, tokens), tokens)
        block = xs_ref[slot].astype(jnp.float32)
        block = jnp.where(listed_ref[slot] > 0, block, 0.0)
        normed_ref[rows, :] = layer_norm(block, gain)

    tile = min(512, width)

    @pl.loop(0, width // tile)
    def _(step):
        cols = pl.ds(pl.multiple_of(step * tile, tile), tile)
        part = jnp.dot(normed_ref[0:tokens, :], wq_ref[:, cols], preferred_element_type=jnp.float32)
        q_ref[:, cols] = part.astype(jnp.bfloat16) * jnp.bfloat16(HEAD_DIM ** (-0.5))

    @pl.loop(0, 2 * width // tile)
    def _(step):
        cols = pl.ds(pl.multiple_of(step * tile, tile), tile)
        from_cols = pl.ds(pl.multiple_of(width + step * tile, tile), tile)
        kv_ref[:, cols] = jnp.dot(
            normed_ref[...], wq_ref[:, from_cols], preferred_element_type=jnp.float32
        ).astype(jnp.bfloat16)

    pair = 2 * HEAD_DIM
    low = lax.broadcasted_iota(jnp.int32, (tokens, pair), 1) < HEAD_DIM
    bias = bias_ref[...]

    @pl.loop(0, width // pair)
    def _(group):
        cols = pl.ds(pl.multiple_of(group * pair, pair), pair)
        value_cols = pl.ds(pl.multiple_of(width + group * pair, pair), pair)
        queries = q_ref[:, cols]
        keys = kv_ref[:, cols]
        values = kv_ref[:, value_cols]
        halves = []
        for mine in (low, jnp.logical_not(low)):
            query = jnp.where(mine, queries, jnp.zeros_like(queries))
            scores = lax.dot_general(
                query, keys, (((1,), (1,)), ((), ())), preferred_element_type=jnp.float32
            ) + bias
            shifted = jnp.exp(scores - jnp.max(scores, axis=-1, keepdims=True))
            total = jnp.sum(shifted, axis=-1, keepdims=True)
            mixed = jnp.dot(shifted.astype(jnp.bfloat16), values, preferred_element_type=jnp.float32)
            halves.append(mixed / total)
        mixed_ref[:, cols] = jnp.where(low, halves[0], halves[1]).astype(jnp.bfloat16)

    @pl.loop(0, width // tile)
    def _(step):
        cols = pl.ds(pl.multiple_of(step * tile, tile), tile)
        projected = jnp.dot(mixed_ref[...], wo_ref[:, cols], preferred_element_type=jnp.float32)
        out_ref[:, cols] = (x_ref[:, cols].astype(jnp.float32) + projected).astype(out_ref.dtype)


def attend(listed, block, others, norm_gain, bias, qkv_weight, out_weight):
    tokens, width = block.shape
    count = (others.shape[0] + 1) * tokens
    vmem = pl.BlockSpec(memory_space=pltpu.VMEM)
    return pl.pallas_call(
        attend_kernel,
        out_shape=jax.ShapeDtypeStruct(block.shape, block.dtype),
        in_specs=[pl.BlockSpec(memory_space=pltpu.SMEM)] + [vmem] * 6,
        out_specs=vmem,
        scratch_shapes=[
            pltpu.VMEM((count, width), jnp.bfloat16),
            pltpu.VMEM((tokens, width), jnp.bfloat16),
            pltpu.VMEM((count, 2 * width), jnp.bfloat16),
            pltpu.VMEM((tokens, width), jnp.bfloat16),
        ],
        compiler_params=pltpu.CompilerParams(vmem_limit_bytes=60 * 1024 * 1024),
        name="attend",
    )(listed, block, others, norm_gain, bias, qkv_weight, out_weight)


def shards(voxels, norm_gain, qkv_weight, out_weight, neighbours):
    block_size, model_width = voxels.shape[-2:]
    block = voxels.reshape(block_size, model_width)
    regions, owners = (lax.axis_size("region"), lax.axis_size("owner"))
    region, owner = (lax.axis_index("region"), lax.axis_index("owner"))
    together = regions == 2 and owners % 4 == 0 and owners > 4
    if together:
        offsets = [(0, -1), (0, 1), (1 - 2 * region, -1), (1 - 2 * region, 1), (1 - 2 * region, 0)]
    else:
        wide = padded(voxels[:, :, 0], (("owner", 1), ("region", 0)), 1)
        wide = wide.reshape(-1, block_size, model_width)
        middle = wide.shape[0] // 2
        others = jnp.concatenate([wide[:middle], wide[middle + 1:]], axis=0)
        full_qkv = lax.all_gather(qkv_weight, ("region", "owner"), axis=0, tiled=True)
        full_out = lax.all_gather(out_weight, ("region", "owner"), axis=0, tiled=True)
        offsets = [(i, j) for i in (-1, 0, 1) for j in (-1, 0, 1) if i or j]
    numbers = []
    for up, along in offsets:
        inside = (owner + along >= 0) & (owner + along < owners)
        number = (region + up) * owners + owner + along
        numbers.append(jnp.where(inside & (number >= 0), number, -2))
    listed = jnp.any(neighbours.reshape(1, -1) == jnp.stack(numbers)[:, None], axis=1)
    present = jnp.concatenate([jnp.ones((1,), bool), listed])
    bias = jnp.repeat(jnp.where(present, 0.0, -1e30).astype(jnp.float32), block_size)[None, :]
    if together:
        out = fused(block, qkv_weight, out_weight, norm_gain[None, :], bias)
        return out.reshape(voxels.shape)
    out = attend(
        listed.astype(jnp.int32), block, others, norm_gain[None, :], bias, full_qkv, full_out
    )
    return out.reshape(voxels.shape)


def solution(mesh):
    return jax.shard_map(
        shards,
        mesh=mesh,
        in_specs=(
            P("region", "owner", None, None, None),
            P(),
            P(("region", "owner"), None),
            P(("region", "owner"), None),
            P("region", "owner", None, None),
        ),
        out_specs=P("region", "owner", None, None, None),
        check_vma=False,
    )
```

time: 107 us -> 125 us (1.17)
  Pallas kernels: 104 us -> 118 us
  local copies, waits for them, and re-layouts: 0.75 us -> 5.35 us
    pallas_call x2 -> x1, Pallas kernels: 104 us -> 118 us  [fused(): pl.pallas_call(functools.partial(fused_kernel, owners), out_shape=jax.Sha...]
    unnamed x2 -> x5, local copies, waits for them, and re-layouts: 0.67 us -> 3.2 us
    reshape x0 -> x3, local copies, waits for them, and re-layouts: none -> 2.06 us  [the longest x2 1.16 us: fused(): parted = qkv_weight.reshape(depth, 3, groups, share).transpose(2, 0, 1, 3)]
where the time goes in v2:
time: 125 us; the launch traced here: 124 us
  Pallas kernels  118 us (94%)
  local copies, waits for them, and re-layouts  5.35 us (4%)
    pallas_call x1, Pallas kernels, fused(): pl.pallas_call(functools.partial(fused_kernel, owners), out_shape=jax.Sha...  118 us
    unnamed x5, local copies, waits for them, and re-layouts  3.2 us

profile of v2, /device:TPU:4, one launch (start us, length us, event | category | flops | bytes accessed | tf_op | source)
XLA Modules:
  0.0 123.9 jit_solution(15600059374006232521)
XLA Ops:
  0.0 0.1 stack.23
  0.1 0.0 copy-start
  0.1 0.7 copy-done
  0.7 0.2 compare_reduce_fusion
  0.9 0.1 add_select_fusion
  1.0 0.1 broadcast_bitcast_fusion
  1.1 0.6 copy.9
  1.7 1.1 reshape.16
  2.7 0.1 copy.11
  2.9 0.9 reshape.17.wq_ref
  3.8 118.2 %fused.1 = bf16[256,1024]{1,0:T(8,128)(2,1)} custom-call(bf16[256,1024]{1,0:T(8,128)(2,1)} %bitcast.18, bf16[4,32,768]{2,1,0:T(8,128)(2,1)} %reshape.17.wq_ref, bf16[32,1024]{1,0:T(8,128)(2,1)} %wo_ref.1, f32[1,1024]{1,0:T(1,128)} %bitcast.20, f32[1,1536]{1,0:T(1,128)} %bitcast.19), custom_call_target="tpu_custom_call" | custom-call | tf_op jit(solution)/shard_map/fused/pallas_call | solution.py:382
  122.0 1.9 %copy.13 = bf16[1,1,1,256,1024]{4,3,2,1,0:T(8,128)(2,1)} copy(bf16[1,1,1,256,1024]{4,3,2,1,0:T(8,128)(2,1)} %bitcast.16) | data formatting | bytes 1048576
Async XLA Ops:
  0.1 0.7 copy-start

commit v3 on v2

--- a/solution.py
+++ b/solution.py
@@ -9,7 +9,7 @@
 
 HEAD_DIM = 64
 MESH = pl.DeviceIdType.MESH
-GROUPS = 4
+GROUPS = 1
 SIB, UP, DOWN, ACROSS, REGION = range(5)
 
 
@@ -228,8 +228,14 @@
     def out_across():
         src = ident(region, plane, 1 - row, core)
         arrive("o", src, None)
-        for kind in (REGION, UP, DOWN, SIB):
+        for kind in (REGION, SIB):
             send("o", kind, src, None)
+
+    def out_line():
+        for y in (row, 1 - row):
+            src = ident(region, plane, y, core)
+            for kind in (UP, DOWN):
+                send("o", kind, src, None, own=y is row)
 
     def out_region():
         for y in (row, 1 - row):
@@ -245,10 +251,6 @@
                 arrive("o", src, cond)
                 for kind in onward + (SIB,):
                     send("o", kind, src, cond)
-
-    def out_own():
-        for kind in (ACROSS, REGION, UP, DOWN, SIB):
-            send("o", kind, me, None, own=True)
 
     gain = gain_ref[...]
 
@@ -297,8 +299,11 @@
     for kind in (UP, DOWN, ACROSS):
         send(0, kind, me, None, own=True)
     send_block(x_ref, 4, targets[REGION], 0, None)
+    send("o", ACROSS, me, None, own=True)
+    send("o", REGION, me, None, own=True)
     for kind in (REGION, SIB):
         send(0, kind, me, None, own=True)
+    send("o", SIB, me, None, own=True)
     send_block(x_ref, 1 - core, side, 1, has_side)
     send_block(x_ref, core, targets[SIB], 2, None)
     local = [
@@ -326,7 +331,7 @@
         norm_block(slot)
 
     first = near_steps(0, own=False)
-    for step in first[:3] + [relay] + first[3:]:
+    for step in first[:1] + [out_across] + first[1:3] + [relay] + first[3:]:
         step()
     norms = [
         functools.partial(norm_step, 1 - core, None),
@@ -335,26 +340,30 @@
         functools.partial(norm_step, 3 - core, None),
         functools.partial(norm_step, 2 + core, has_side),
     ]
-    interleave(norms, near_steps(1))
+    interleave(norms, near_steps(1) if groups > 1 else [])
     for copy in local:
         copy.wait()
+    out_line()
+    out_region()
     for step in far_steps(0):
         step()
-    out_steps = [out_own, out_across, out_region] + [
-        functools.partial(out_plane, d) for d in range(1, planes)
-    ] + [functools.partial(sibling_step, "o")]
-    half = len(out_steps) // 2
+    late = [functools.partial(out_plane, d) for d in range(1, planes)]
     for g in range(groups):
-        steps = []
-        if g + 2 < groups:
-            steps += near_steps(g + 2)
-        if g + 2 == groups:
-            steps += out_steps[:half]
-        if g + 1 < groups:
-            steps += far_steps(g + 1)
-        if g + 1 == groups:
-            steps += out_steps[half:]
-        interleave(compute_steps(g), steps)
+        pieces = compute_steps(g)
+        if g == 0:
+            middle = len(pieces) // 3
+            for piece in pieces[:middle]:
+                piece()
+            interleave(pieces[middle:], late)
+        else:
+            for step in far_steps(g):
+                step()
+            for piece in pieces:
+                piece()
+        if 0 < g < groups - 1:
+            for step in near_steps(g + 1):
+                step()
+    sibling_step("o")
 
     tile = min(512, width)
     for at in range(0, width, tile):

time: 125 us -> 89.3 us (0.71)
  Pallas kernels: 118 us -> 85.6 us
  local copies, waits for them, and re-layouts: 5.35 us -> 3.29 us
    pallas_call x1, Pallas kernels: 118 us -> 85.6 us  [fused(): pl.pallas_call(functools.partial(fused_kernel, owners), out_shape=jax.Sha...]
    reshape x3 -> x0, local copies, waits for them, and re-layouts: 2.06 us -> none  [the longest x2 1.16 us: fused(): parted = qkv_weight.reshape(depth, 3, groups, share).transpose(2, 0, 1, 3)]
where the time goes in v3:
time: 89.3 us; the launch traced here: 89.1 us
  Pallas kernels  85.6 us (96%)
  local copies, waits for them, and re-layouts  3.29 us (4%)
    pallas_call x1, Pallas kernels, fused(): pl.pallas_call(functools.partial(fused_kernel, owners), out_shape=jax.Sha...  85.6 us
    unnamed x5, local copies, waits for them, and re-layouts  3.2 us

profile of v3, /device:TPU:4, one launch (start us, length us, event | category | flops | bytes accessed | tf_op | source)
XLA Modules:
  0.0 89.1 jit_solution(9145279130352527686)
XLA Ops:
  0.0 0.1 stack.23
  0.1 0.0 copy-start
  0.1 0.7 copy-done
  0.7 0.2 compare_reduce_fusion
  0.9 0.1 add_select_fusion
  1.0 0.1 broadcast_bitcast_fusion
  1.1 0.6 copy.6
  1.7 85.6 %fused.1 = bf16[256,1024]{1,0:T(8,128)(2,1)} custom-call(bf16[256,1024]{1,0:T(8,128)(2,1)} %bitcast.15, bf16[1,32,3072]{2,1,0:T(8,128)(2,1)} %bitcast.16, bf16[32,1024]{1,0:T(8,128)(2,1)} %wo_ref.1, f32[1,1024]{1,0:T(1,128)} %bitcast.18, f32[1,1536]{1,0:T(1,128)} %bitcast.17), custom_call_target="tpu_custom_call" | custom-call | tf_op jit(solution)/shard_map/fused/pallas_call | solution.py:391
  87.3 1.9 %copy.8 = bf16[1,1,1,256,1024]{4,3,2,1,0:T(8,128)(2,1)} copy(bf16[1,1,1,256,1024]{4,3,2,1,0:T(8,128)(2,1)} %bitcast.14) | data formatting | bytes 1048576
Async XLA Ops:
  0.1 0.7 copy-start
